TPU v7x, 32 devices: a whole 2x2x4 slice. The times are simulated.
32 devices in a mesh: row: 8 (over y, x, core), col: 4 (over z).
Axes of the slice: x: 2, y: 2, z: 4, core: 2. Of those that a mesh axis runs over, the one named last changes fastest.
Arguments:
- final_amp: bfloat16 [8, 32, 128, 440], P('row', 'col'), may hold values from -0.19921875 to 0.19921875
- initial_amp: bfloat16 [4, 32, 128, 440], P('col', 'row'), may hold values from -0.19921875 to 0.19921875
- pair_final: int32 [8, 4, 128], P('row', 'col'), may hold values from 0 to 31
- pair_initial: int32 [8, 4, 128], P('row', 'col'), may hold values from 0 to 31
- map_final: int32 [8, 32, 440], P('row', 'col'), may hold values from 0 to 439, each once within a row
- map_initial: int32 [4, 32, 440], P('col', 'row'), may hold values from 0 to 439, each once within a row
- counts: int32 [8, 4], P('row', 'col'), may hold values from 16 to 128, as said below
Outputs:
- density: float32 [440, 440], replicated
Inputs may be any that keep to these rules, and one draw needn't show every extreme that they name: `counts`: slots at or past a cell's count are ignored. Exactly one cell of every draw has 128 live slots.
All inputs are finite; a program needn't handle non-finite values.
Results may differ from a plain program's by a relative error of at most 0.0003.
Values may be sent and summed in bfloat16 or wider, within the bound.
A program may use at most 64 MiB of HBM per device.

v0:
```python
import jax
import jax.numpy as jnp
from jax import lax
from jax.sharding import PartitionSpec as P

GROUP = 32


def permute_columns(blocks, orbital_map):
    return jnp.take(blocks, orbital_map, axis=1)


def shards(final_amp, initial_amp, pair_final, pair_initial, map_final, map_initial, counts):
    own_final = jax.vmap(permute_columns)(final_amp[0], map_final[0])[None]
    own_initial = jax.vmap(permute_columns)(initial_amp[0], map_initial[0])[None]
    row_seg = lax.all_gather(own_final, "col", axis=1, tiled=True)[0]
    column_seg = lax.all_gather(own_initial, "row", axis=1, tiled=True)[0]
    slots_final = pair_final[0, 0]
    slots_initial = pair_initial[0, 0]
    live_count = counts[0, 0]
    orbitals = final_amp.shape[3]
    group_size = GROUP

    def advance(index, summed):
        first_slot = index * group_size
        which_final = lax.dynamic_slice_in_dim(slots_final, first_slot, group_size)
        which_initial = lax.dynamic_slice_in_dim(slots_initial, first_slot, group_size)
        live_mask = first_slot + jnp.arange(group_size, dtype=jnp.int32) < live_count
        left = jnp.take(row_seg, which_final, axis=0)
        right = jnp.take(column_seg, which_initial, axis=0)
        left = jnp.where(live_mask[:, None, None], left, jnp.zeros_like(left))
        product = lax.dot_general(
            left.reshape(-1, orbitals),
            right.reshape(-1, orbitals),
            (((0,), (0,)), ((), ())),
            preferred_element_type=jnp.float32,
        )
        return summed + product

    turns = (live_count + group_size - 1) // group_size
    partial_density = lax.fori_loop(0, turns, advance, jnp.zeros((orbitals, orbitals), jnp.float32))
    band = lax.psum_scatter(partial_density, "col", scatter_dimension=0, tiled=True)
    band = lax.psum(band, "row")
    density = lax.all_gather(band, "col", axis=0, tiled=True)
    return density


def solution(mesh):
    placed = (
        P("row", "col", None, None),
        P("col", "row", None, None),
        P("row", "col", None),
        P("row", "col", None),
        P("row", "col", None),
        P("col", "row", None),
        P("row", "col"),
    )
    return jax.shard_map(shards, mesh=mesh, in_specs=placed, out_specs=P(), check_vma=False)
```

profile of v0, /device:TPU:0, one launch (start us, length us, event | category | flops | bytes accessed | tf_op | source)
XLA Modules:
  0.0 321.1 jit_solution(12124861493017973160)
XLA Ops:
  6.5 0.8 fusion.18
  7.3 0.7 compare_and_fusion.2
  8.2 30.8 %gather_fusion.2 = bf16[3520,128]{1,0:T(8,128)(2,1)S(1)} fusion(bf16[8,128,440]{1,2,0:T(8,128)(2,1)S(1)} %bitcast.44, s32[3520]{0:T(1024)S(1)} %reshape.110), kind=kCustom, calls=%fused_computation.2 | custom fusion | bytes 1830400 | tf_op jit(solution)/shard_map/vmap(jit(_take))/gather | solution.py:10
  39.0 1.4 broadcast_select_fusion
  40.5 15.7 %gather_fusion.3 = bf16[1760,128]{1,0:T(8,128)(2,1)S(1)} fusion(bf16[4,128,440]{1,2,0:T(8,128)(2,1)S(1)} %bitcast.45, s32[1760]{0:T(1024)S(1)} %reshape.116), kind=kCustom, calls=%fused_computation.3 | custom fusion | bytes 915200 | tf_op jit(solution)/shard_map/vmap(jit(_take))/gather | solution.py:10
  56.3 1.1 broadcast_select_fusion.1
  58.2 56.1 %all-gather.4.cloned.1.call-done = bf16[1,32,128,440]{2,3,0,1:T(8,128)(2,1)} async-done(((bf16[1,8,128,440]{2,3,0,1:T(8,128)(2,1)}), bf16[1,32,128,440]{2,3,0,1:T(8,128)(2,1)}) %all-gather.4.cloned.1.call-update) | async-done | bytes 3604496 | tf_op jit(solution)/shard_map/all_gather | solution.py:16
  114.3 6.4 %copy.18 = bf16[32,128,440]{2,1,0:T(8,128)(2,1)} copy(bf16[32,128,440]{1,2,0:T(8,128)(2,1)} %bitcast.47) | data formatting | bytes 7208960 | tf_op jit(solution)/shard_map/while | solution.py:41
  120.7 28.2 %all-gather.6.cloned.1.call-done = bf16[1,32,128,440]{2,3,0,1:T(8,128)(2,1)} async-done(((bf16[1,4,128,440]{2,3,0,1:T(8,128)(2,1)}), bf16[1,32,128,440]{2,3,0,1:T(8,128)(2,1)}) %all-gather.6.cloned.1.call-update) | async-done | bytes 3604496 | tf_op jit(solution)/shard_map/all_gather | solution.py:17
  148.9 6.5 %copy.19 = bf16[32,128,440]{2,1,0:T(8,128)(2,1)} copy(bf16[32,128,440]{1,2,0:T(8,128)(2,1)} %bitcast.48) | data formatting | bytes 7208960 | tf_op jit(solution)/shard_map/while | solution.py:41
  155.3 0.1 broadcast_in_dim.43
  155.5 33.5 %while.10 = (s32[]{:T(128)}, f32[440,440]{1,0:T(8,128)S(1)}, s32[]{:T(128)}, s32[]{:T(128)}, s32[128]{0:T(128)S(1)}, /*index=5*/bf16[32,128,440]{2,1,0:T(8,128)(...) while((s32[]{:T(128)}, f32[440,440]{1,0:T(8,128)S(1)}, ...), condition=%wide.region_1.3_spmd, body=%wide.region_0.0_spmd.sunk | while | flops 1591574016 | bytes 23185264 | solution.py:41
  155.5 0.1 compare_and_fusion.5
  155.6 5.0 %gather_fusion = bf16[32,128,440]{2,1,0:T(8,128)(2,1)} fusion(bf16[32,128,440]{2,1,0:T(8,128)(2,1)} %get-tuple-element.169, s32[1024]{0:T(1024)S(1)} %pad_clamp_fusion.4), kind=kCustom, calls=%fused_computation.1.clone.clone.1 | custom fusion | bytes 7209088 | tf_op jit(solution)/shard_map/while/body/jit(_take)/gather | solution.py:30
  160.6 4.9 %gather_fusion.1 = bf16[32,128,440]{2,1,0:T(8,128)(2,1)} fusion(bf16[32,128,440]{2,1,0:T(8,128)(2,1)} %get-tuple-element.167, s32[1024]{0:T(1024)S(1)} %pad_clamp_fusion.5), kind=kCustom, calls=%fused_computation.clone.clone.1 | custom fusion | bytes 7209088 | tf_op jit(solution)/shard_map/while/body/jit(_take)/gather | solution.py:29
  165.5 0.7 add_compare_fusion.2
  166.1 6.1 %fusion.25 = f32[440,440]{1,0:T(8,128)S(1)} fusion(f32[440,440]{1,0:T(8,128)S(1)} %get-tuple-element.151, bf16[32,128,440]{2,1,0:T(8,128)(2,1)} %gather_fusion, pred[32]{0:T(512)(128)(4,1)S(1)} %get-tuple-element.135, bf16[32,128,440]{2,1,0:T(8,128)(2,1)} %gather_fusion.1, pred[32]{0:T(512)(128)(4,1)S(1)} %get-tuple-element.137, ...), kind=kOutput, calls=%fused_computation.13.clone.1 | convolution fusion | flops 1591571456 | bytes 8757856 | tf_op jit(solution)/shard_map/while/body/dot_general | solution.py:32
  172.3 5.0 %gather_fusion = bf16[32,128,440]{2,1,0:T(8,128)(2,1)} fusion(bf16[32,128,440]{2,1,0:T(8,128)(2,1)} %get-tuple-element.169, s32[1024]{0:T(1024)S(1)} %pad_clamp_fusion.4), kind=kCustom, calls=%fused_computation.1.clone.clone.1 | custom fusion | bytes 7209088 | tf_op jit(solution)/shard_map/while/body/jit(_take)/gather | solution.py:30
  177.3 4.9 %gather_fusion.1 = bf16[32,128,440]{2,1,0:T(8,128)(2,1)} fusion(bf16[32,128,440]{2,1,0:T(8,128)(2,1)} %get-tuple-element.167, s32[1024]{0:T(1024)S(1)} %pad_clamp_fusion.5), kind=kCustom, calls=%fused_computation.clone.clone.1 | custom fusion | bytes 7209088 | tf_op jit(solution)/shard_map/while/body/jit(_take)/gather | solution.py:29
  182.2 0.7 add_compare_fusion.2
  182.9 6.1 %fusion.25 = f32[440,440]{1,0:T(8,128)S(1)} fusion(f32[440,440]{1,0:T(8,128)S(1)} %get-tuple-element.151, bf16[32,128,440]{2,1,0:T(8,128)(2,1)} %gather_fusion, pred[32]{0:T(512)(128)(4,1)S(1)} %get-tuple-element.135, bf16[32,128,440]{2,1,0:T(8,128)(2,1)} %gather_fusion.1, pred[32]{0:T(512)(128)(4,1)S(1)} %get-tuple-element.137, ...), kind=kOutput, calls=%fused_computation.13.clone.1 | convolution fusion | flops 1591571456 | bytes 8757856 | tf_op jit(solution)/shard_map/while/body/dot_general | solution.py:32
  188.9 22.8 %fusion = f32[112,440]{1,0:T(8,128)S(1)} fusion(f32[440,440]{1,0:T(8,128)S(1)} %get-tuple-element.49), kind=kCustom, calls=%all-reduce-scatter | all-reduce-scatter fusion | flops 197121 | bytes 972032
  211.7 2.1 collective-permute-start
  213.9 0.6 dynamic-slice.4
  215.1 0.2 collective-permute-done
  215.3 0.2 concatenate.6
  215.6 0.7 constant_dynamic-slice_fusion
  216.3 74.9 %all-reduce.4.cloned.1.call-done = f32[110,440]{1,0:T(8,128)} async-done(((f32[110,440]{1,0:T(8,128)}), f32[110,440]{1,0:T(8,128)}) %all-reduce.4.cloned.1.call-update) | async-done | bytes 193616 | tf_op jit(solution)/shard_map/psum | solution.py:43
  291.2 1.1 copy.20
  292.3 20.9 %all-gather = f32[4,110,440]{1,2,0:T(8,128)S(1)} all-gather(f32[1,110,440]{1,2,0:T(8,128)S(1)} %copy.20), channel_id=1, replica_groups=mesh['row'=8,'col'=4] {'col'}, dimensions={0}, use_global_device_ids=true | all-gather | bytes 968000 | tf_op jit(solution)/shard_map/all_gather | solution.py:44
  313.2 0.4 copy.21
  313.6 1.0 reshape.125
  (28 shorter events, 0.5 us)
Async XLA Ops:
  6.5 1.6 copy-start
  6.5 107.7 %all-gather.4.cloned.1.call-start = ((), (), s32[]{:S(2)}) async-start(), calls=%async_computation | async-start | bytes 4505600 | tf_op jit(solution)/shard_map/all_gather | solution.py:16
  8.2 32.3 %copy-start.2 = (s32[1,4,440]{2,1,0:T(4,128)S(1)}, s32[1,4,440]{2,1,0:T(4,128)}, u32[]{:S(2)}) copy-start(s32[1,4,440]{2,1,0:T(4,128)} %param.16) | copy-start | bytes 21124
  8.2 32.4 %copy-start.1 = (bf16[1,4,128,440]{2,3,1,0:T(8,128)(2,1)S(1)}, bf16[1,4,128,440]{2,3,1,0:T(8,128)(2,1)}, u32[]{:S(2)}) copy-start(bf16[1,4,128,440]{2,3,1,0:T(8,128)(2,1)} %param.12) | copy-start | bytes 1351684
  40.4 108.5 %all-gather.6.cloned.1.call-start = ((), (), s32[]{:S(2)}) async-start(), calls=%async_computation.1 | async-start | bytes 4055040 | tf_op jit(solution)/shard_map/all_gather | solution.py:17
  57.4 233.8 %all-reduce.4.cloned.1.call-start = ((), (), s32[]{:S(2)}) async-start(), calls=%async_computation.2 | async-start | bytes 458752 | tf_op jit(solution)/shard_map/psum | solution.py:43
  148.9 6.6 %copy-start.3 = (s32[1,1,128]{2,1,0:T(1,128)S(1)}, s32[1,1,128]{2,1,0:T(1,128)}, u32[]{:S(2)}) copy-start(s32[1,1,128]{2,1,0:T(1,128)} %param.13) | copy-start | bytes 1540
  148.9 6.6 %copy-start.4 = (s32[1,1,128]{2,1,0:T(1,128)S(1)}, s32[1,1,128]{2,1,0:T(1,128)}, u32[]{:S(2)}) copy-start(s32[1,1,128]{2,1,0:T(1,128)} %param.14) | copy-start | bytes 1540
  155.5 58.4 %copy-start.5 = (u32[32]{0:T(128)S(1)}, u32[32]{0:T(128)}, u32[]{:S(2)}) copy-start(u32[32]{0:T(128)} %constant.104) | copy-start | bytes 388
  211.7 3.6 %collective-permute-start = (f32[6,440]{1,0:T(8,128)S(1)}, f32[6,440]{1,0:T(8,128)S(1)}, u32[]{:S(2)}, u32[]{:S(2)}) collective-permute-start(f32[6,440]{1,0:T(8,128)S(1)} %slice.8), channel_id=1, source_target_pairs={{0,1},{1,2},{2,3},{4,5},{5,6},{6,7},{8,9},{9,10},{10,11},{12,13},{... | collective-permute-start | bytes 31688
Sparse Core Ops, SparseCore 0:
  40.5 73.7 all-gather.3
  116.2 32.6 all-gather.5
  216.4 74.7 all-reduce.3
where the time goes:
time: 322 us; the launch traced here: 321 us
  waiting for transfers between devices  159 us (49%)
  local copies, waits for them, and re-layouts  83.4 us (26%)
  blocking collectives  43.7 us (14%)
  between operations  14.6 us (5%)
  matrix products  12.1 us (4%)
  other arithmetic  5.57 us (2%)
    psum x1, waiting for transfers between devices, shards(): band = lax.psum(band, 'row')  74.9 us
    all_gather x1, waiting for transfers between devices, shards(): row_seg = lax.all_gather(own_final, 'col', axis=1, tiled=True)[0]  56.1 us
    gather x4, local copies, waits for them, and re-layouts, permute_columns(): return jnp.take(blocks, orbital_map, axis=1)  46.6 us
    all_gather x1, waiting for transfers between devices, shards(): column_seg = lax.all_gather(own_initial, 'row', axis=1, tiled=True)[0]  28.2 us
    unnamed x1, blocking collectives  22.8 us
    all_gather x1, blocking collectives, shards(): density = lax.all_gather(band, 'col', axis=0, tiled=True)  20.9 us
    while x2, local copies, waits for them, and re-layouts, shards(): lax.fori_loop(0, turns, advance, jnp.zeros((orbitals, orbitals), jnp.floa...  12.9 us
    dot_general x2, matrix products, advance(): lax.dot_general(left.reshape(-1, orbitals), right.reshape(-1, orbitals),...  12.1 us
  transfers between devices with their start and end apart: 4, of which 4 were waited for; matrix products, arithmetic and copies ran while one was open for 7% of the time, Pallas kernels for 0%

commit v1 on v0

--- a/solution.py
+++ b/solution.py
@@ -41,7 +41,9 @@
     partial_density = lax.fori_loop(0, turns, advance, jnp.zeros((orbitals, orbitals), jnp.float32))
     band = lax.psum_scatter(partial_density, "col", scatter_dimension=0, tiled=True)
     band = lax.psum(band, "row")
-    density = lax.all_gather(band, "col", axis=0, tiled=True)
+    density = jnp.concatenate(
+        lax.all_to_all(jnp.stack([band] * lax.axis_size("col")), "col", 0, 0), axis=0
+    )
     return density
 
 

time: 322 us -> 329 us (1.022)
  blocking collectives: 43.7 us -> 50.4 us
    all_to_all x0 -> x1, blocking collectives: none -> 27.6 us  [shards(): lax.all_to_all(jnp.stack([band] * lax.axis_size('col')), 'col', 0, 0)]
    all_gather x1 -> x0, blocking collectives: 20.9 us -> none  [shards(): density = lax.all_gather(band, 'col', axis=0, tiled=True)]
where the time goes in v1:
time: 329 us; the launch traced here: 328 us
  waiting for transfers between devices  159 us (48%)
  local copies, waits for them, and re-layouts  83.5 us (25%)
  blocking collectives  50.4 us (15%)
  between operations  14.6 us (4%)
  matrix products  12.1 us (4%)
  other arithmetic  5.57 us (2%)
    psum x1, waiting for transfers between devices, shards(): band = lax.psum(band, 'row')  74.9 us
    all_gather x1, waiting for transfers between devices, shards(): row_seg = lax.all_gather(own_final, 'col', axis=1, tiled=True)[0]  56.1 us
    gather x4, local copies, waits for them, and re-layouts, permute_columns(): return jnp.take(blocks, orbital_map, axis=1)  46.6 us
    all_gather x1, waiting for transfers between devices, shards(): column_seg = lax.all_gather(own_initial, 'row', axis=1, tiled=True)[0]  28.2 us
    all_to_all x1, blocking collectives, shards(): lax.all_to_all(jnp.stack([band] * lax.axis_size('col')), 'col', 0, 0)  27.6 us
    unnamed x1, blocking collectives  22.8 us
    while x2, local copies, waits for them, and re-layouts, shards(): lax.fori_loop(0, turns, advance, jnp.zeros((orbitals, orbitals), jnp.floa...  12.9 us
    dot_general x2, matrix products, advance(): lax.dot_general(left.reshape(-1, orbitals), right.reshape(-1, orbitals),...  12.1 us
  transfers between devices with their start and end apart: 4, of which 4 were waited for; matrix products, arithmetic and copies ran while one was open for 7% of the time, Pallas kernels for 0%

profile of v1, /device:TPU:0, one launch (start us, length us, event | category | flops | bytes accessed | tf_op | source)
XLA Modules:
  0.0 327.8 jit_solution(6601023183896258490)
XLA Ops:
  6.5 0.8 fusion.18
  7.3 0.7 compare_and_fusion.2
  8.2 30.8 %gather_fusion.2 = bf16[3520,128]{1,0:T(8,128)(2,1)S(1)} fusion(bf16[8,128,440]{1,2,0:T(8,128)(2,1)S(1)} %bitcast.43, s32[3520]{0:T(1024)S(1)} %reshape.116), kind=kCustom, calls=%fused_computation.2 | custom fusion | bytes 1830400 | tf_op jit(solution)/shard_map/vmap(jit(_take))/gather | solution.py:10
  39.0 1.4 broadcast_select_fusion
  40.5 15.7 %gather_fusion.3 = bf16[1760,128]{1,0:T(8,128)(2,1)S(1)} fusion(bf16[4,128,440]{1,2,0:T(8,128)(2,1)S(1)} %bitcast.44, s32[1760]{0:T(1024)S(1)} %reshape.122), kind=kCustom, calls=%fused_computation.3 | custom fusion | bytes 915200 | tf_op jit(solution)/shard_map/vmap(jit(_take))/gather | solution.py:10
  56.3 1.1 broadcast_select_fusion.1
  58.2 56.1 %all-gather.3.cloned.1.call-done = bf16[1,32,128,440]{2,3,0,1:T(8,128)(2,1)} async-done(((bf16[1,8,128,440]{2,3,0,1:T(8,128)(2,1)}), bf16[1,32,128,440]{2,3,0,1:T(8,128)(2,1)}) %all-gather.3.cloned.1.call-update) | async-done | bytes 3604496 | tf_op jit(solution)/shard_map/all_gather | solution.py:16
  114.3 6.4 %copy.18 = bf16[32,128,440]{2,1,0:T(8,128)(2,1)} copy(bf16[32,128,440]{1,2,0:T(8,128)(2,1)} %bitcast.46) | data formatting | bytes 7208960 | tf_op jit(solution)/shard_map/while | solution.py:41
  120.7 28.2 %all-gather.5.cloned.1.call-done = bf16[1,32,128,440]{2,3,0,1:T(8,128)(2,1)} async-done(((bf16[1,4,128,440]{2,3,0,1:T(8,128)(2,1)}), bf16[1,32,128,440]{2,3,0,1:T(8,128)(2,1)}) %all-gather.5.cloned.1.call-update) | async-done | bytes 3604496 | tf_op jit(solution)/shard_map/all_gather | solution.py:17
  148.9 6.5 %copy.19 = bf16[32,128,440]{2,1,0:T(8,128)(2,1)} copy(bf16[32,128,440]{1,2,0:T(8,128)(2,1)} %bitcast.47) | data formatting | bytes 7208960 | tf_op jit(solution)/shard_map/while | solution.py:41
  155.3 0.1 broadcast_in_dim.43
  155.5 33.5 %while.10 = (s32[]{:T(128)}, f32[440,440]{1,0:T(8,128)S(1)}, s32[]{:T(128)}, s32[]{:T(128)}, s32[128]{0:T(128)S(1)}, /*index=5*/bf16[32,128,440]{2,1,0:T(8,128)(...) while((s32[]{:T(128)}, f32[440,440]{1,0:T(8,128)S(1)}, ...), condition=%wide.region_1.3_spmd, body=%wide.region_0.0_spmd.sunk | while | flops 1591574016 | bytes 23185264 | solution.py:41
  155.5 0.1 compare_and_fusion.5
  155.6 5.0 %gather_fusion = bf16[32,128,440]{2,1,0:T(8,128)(2,1)} fusion(bf16[32,128,440]{2,1,0:T(8,128)(2,1)} %get-tuple-element.169, s32[1024]{0:T(1024)S(1)} %pad_clamp_fusion.4), kind=kCustom, calls=%fused_computation.1.clone.clone.1 | custom fusion | bytes 7209088 | tf_op jit(solution)/shard_map/while/body/jit(_take)/gather | solution.py:30
  160.6 4.9 %gather_fusion.1 = bf16[32,128,440]{2,1,0:T(8,128)(2,1)} fusion(bf16[32,128,440]{2,1,0:T(8,128)(2,1)} %get-tuple-element.167, s32[1024]{0:T(1024)S(1)} %pad_clamp_fusion.5), kind=kCustom, calls=%fused_computation.clone.clone.1 | custom fusion | bytes 7209088 | tf_op jit(solution)/shard_map/while/body/jit(_take)/gather | solution.py:29
  165.5 0.7 add_compare_fusion.2
  166.1 6.1 %fusion.25 = f32[440,440]{1,0:T(8,128)S(1)} fusion(f32[440,440]{1,0:T(8,128)S(1)} %get-tuple-element.151, bf16[32,128,440]{2,1,0:T(8,128)(2,1)} %gather_fusion, pred[32]{0:T(512)(128)(4,1)S(1)} %get-tuple-element.135, bf16[32,128,440]{2,1,0:T(8,128)(2,1)} %gather_fusion.1, pred[32]{0:T(512)(128)(4,1)S(1)} %get-tuple-element.137, ...), kind=kOutput, calls=%fused_computation.13.clone.1 | convolution fusion | flops 1591571456 | bytes 8757856 | tf_op jit(solution)/shard_map/while/body/dot_general | solution.py:32
  172.3 5.0 %gather_fusion = bf16[32,128,440]{2,1,0:T(8,128)(2,1)} fusion(bf16[32,128,440]{2,1,0:T(8,128)(2,1)} %get-tuple-element.169, s32[1024]{0:T(1024)S(1)} %pad_clamp_fusion.4), kind=kCustom, calls=%fused_computation.1.clone.clone.1 | custom fusion | bytes 7209088 | tf_op jit(solution)/shard_map/while/body/jit(_take)/gather | solution.py:30
  177.3 4.9 %gather_fusion.1 = bf16[32,128,440]{2,1,0:T(8,128)(2,1)} fusion(bf16[32,128,440]{2,1,0:T(8,128)(2,1)} %get-tuple-element.167, s32[1024]{0:T(1024)S(1)} %pad_clamp_fusion.5), kind=kCustom, calls=%fused_computation.clone.clone.1 | custom fusion | bytes 7209088 | tf_op jit(solution)/shard_map/while/body/jit(_take)/gather | solution.py:29
  182.2 0.7 add_compare_fusion.2
  182.9 6.1 %fusion.25 = f32[440,440]{1,0:T(8,128)S(1)} fusion(f32[440,440]{1,0:T(8,128)S(1)} %get-tuple-element.151, bf16[32,128,440]{2,1,0:T(8,128)(2,1)} %gather_fusion, pred[32]{0:T(512)(128)(4,1)S(1)} %get-tuple-element.135, bf16[32,128,440]{2,1,0:T(8,128)(2,1)} %gather_fusion.1, pred[32]{0:T(512)(128)(4,1)S(1)} %get-tuple-element.137, ...), kind=kOutput, calls=%fused_computation.13.clone.1 | convolution fusion | flops 1591571456 | bytes 8757856 | tf_op jit(solution)/shard_map/while/body/dot_general | solution.py:32
  188.9 22.8 %fusion = f32[112,440]{1,0:T(8,128)S(1)} fusion(f32[440,440]{1,0:T(8,128)S(1)} %get-tuple-element.49), kind=kCustom, calls=%all-reduce-scatter | all-reduce-scatter fusion | flops 197121 | bytes 972032
  211.7 2.1 collective-permute-start
  213.9 0.6 dynamic-slice.4
  215.1 0.2 collective-permute-done
  215.3 0.2 concatenate.6
  215.6 0.7 constant_dynamic-slice_fusion
  216.3 74.9 %all-reduce.4.cloned.1.call-done = f32[110,440]{1,0:T(8,128)} async-done(((f32[110,440]{1,0:T(8,128)}), f32[110,440]{1,0:T(8,128)}) %all-reduce.4.cloned.1.call-update) | async-done | bytes 193616 | tf_op jit(solution)/shard_map/psum | solution.py:43
  291.2 1.1 copy.20
  292.3 27.6 %all_to_all.5 = f32[4,110,440]{1,2,0:T(8,128)S(1)} all-to-all(f32[4,110,440]{1,2,0:T(8,128)S(1)} %stack.2), channel_id=1, replica_groups=mesh['row'=8,'col'=4] {'col'}, dimensions={0} | all-to-all | bytes 1548800 | tf_op jit(solution)/shard_map/all_to_all | solution.py:45
  319.9 0.4 copy.21
  320.3 1.0 reshape.99
  (29 shorter events, 0.5 us)
Async XLA Ops:
  6.5 1.6 copy-start
  6.5 107.7 %all-gather.3.cloned.1.call-start = ((), (), s32[]{:S(2)}) async-start(), calls=%async_computation.1 | async-start | bytes 4505600 | tf_op jit(solution)/shard_map/all_gather | solution.py:16
  8.2 32.3 %copy-start.2 = (s32[1,4,440]{2,1,0:T(4,128)S(1)}, s32[1,4,440]{2,1,0:T(4,128)}, u32[]{:S(2)}) copy-start(s32[1,4,440]{2,1,0:T(4,128)} %param.16) | copy-start | bytes 21124
  8.2 32.4 %copy-start.1 = (bf16[1,4,128,440]{2,3,1,0:T(8,128)(2,1)S(1)}, bf16[1,4,128,440]{2,3,1,0:T(8,128)(2,1)}, u32[]{:S(2)}) copy-start(bf16[1,4,128,440]{2,3,1,0:T(8,128)(2,1)} %param.12) | copy-start | bytes 1351684
  40.4 108.5 %all-gather.5.cloned.1.call-start = ((), (), s32[]{:S(2)}) async-start(), calls=%async_computation.2 | async-start | bytes 4055040 | tf_op jit(solution)/shard_map/all_gather | solution.py:17
  57.4 233.8 %all-reduce.4.cloned.1.call-start = ((), (), s32[]{:S(2)}) async-start(), calls=%async_computation.3 | async-start | bytes 458752 | tf_op jit(solution)/shard_map/psum | solution.py:43
  148.9 6.6 %copy-start.3 = (s32[1,1,128]{2,1,0:T(1,128)S(1)}, s32[1,1,128]{2,1,0:T(1,128)}, u32[]{:S(2)}) copy-start(s32[1,1,128]{2,1,0:T(1,128)} %param.13) | copy-start | bytes 1540
  148.9 6.6 %copy-start.4 = (s32[1,1,128]{2,1,0:T(1,128)S(1)}, s32[1,1,128]{2,1,0:T(1,128)}, u32[]{:S(2)}) copy-start(s32[1,1,128]{2,1,0:T(1,128)} %param.14) | copy-start | bytes 1540
  155.5 58.4 %copy-start.5 = (u32[32]{0:T(128)S(1)}, u32[32]{0:T(128)}, u32[]{:S(2)}) copy-start(u32[32]{0:T(128)} %constant.104) | copy-start | bytes 388
  211.7 3.6 %collective-permute-start = (f32[6,440]{1,0:T(8,128)S(1)}, f32[6,440]{1,0:T(8,128)S(1)}, u32[]{:S(2)}, u32[]{:S(2)}) collective-permute-start(f32[6,440]{1,0:T(8,128)S(1)} %slice.8), channel_id=1, source_target_pairs={{0,1},{1,2},{2,3},{4,5},{5,6},{6,7},{8,9},{9,10},{10,11},{12,13},{... | collective-permute-start | bytes 31688
Sparse Core Ops, SparseCore 0:
  40.5 73.7 all-gather.2
  116.2 32.6 all-gather.4
  216.4 74.7 all-reduce.3
